TPU v7x, 32 devices: a whole 2x2x4 slice. The times are simulated.
32 devices in a mesh: grp: 2 (over y), tm: 2 (over core), row: 8 (over z, x).
Axes of the slice: x: 2, y: 2, z: 4, core: 2. Of those that a mesh axis runs over, the one named last changes fastest.
Arguments:
- inputs: bfloat16 [8, 8, 43008], P(('grp', 'tm'), 'row'), parts along dimension 0, may hold values from -6 to 6
- weight: bfloat16 [5184, 192], replicated, may hold values from -0.078125 to 0.078125
- cotangent: bfloat16 [8, 8, 43008], P(('grp', 'tm'), 'row'), parts along dimension 0, may hold values from -6 to 6
Outputs:
- output: bfloat16 [8, 8, 43008], P(('grp', 'tm'), 'row'), parts along dimension 0
- input_grad: bfloat16 [8, 8, 43008], P(('grp', 'tm'), 'row'), parts along dimension 0
- filter_grad: bfloat16 [1990656], P(('grp', 'tm', 'row')), parts along dimension 0
There are 2 independent parts, one for each index of `grp`. A program takes and returns all parts, laid end to end along the dimension named above; an argument that names none is the same for every part. Nothing has to cross between parts.
All inputs are finite; a program needn't handle non-finite values.
Results may differ from a plain program's by a relative error of at most 0.0051.
Values may be sent and summed in bfloat16 or wider, within the bound.
A program may use at most 64 MiB of HBM per device.

v0:
```python
import jax
import jax.numpy as jnp
from jax import lax
from jax.sharding import PartitionSpec as P

CH = 192
WIDTH = 224


def passed_along(array, axis, by):
    length = lax.axis_size(axis)
    pairs = [(i, i + by) for i in range(length) if 0 <= i + by < length]
    return lax.ppermute(array, axis, pairs)


def with_halo(array, sides, width):
    for axis, dim in sides:
        size, length = (lax.axis_size(axis), array.shape[dim])
        up = [(i, (i + 1) % size) for i in range(size - 1)]
        down = [(j, i) for i, j in up]
        last = lax.slice_in_dim(array, length - width, length, axis=dim)
        first = lax.slice_in_dim(array, 0, width, axis=dim)
        before = lax.ppermute(last, axis, up)
        after = lax.ppermute(first, axis, down)
        array = jnp.concatenate([before, array, after], axis=dim)
    return array


def on_device(inputs, weight, cotangent):
    frames = inputs.shape[0]
    rows = inputs.shape[1]
    act = jax.nn.silu(inputs.astype(jnp.float32)).astype(jnp.bfloat16)
    earlier = passed_along(act, "tm", 1)
    extended = jnp.concatenate([earlier, act], 0)
    extended = with_halo(extended, (("row", 1),), 1)
    extended = extended.reshape(frames + 2, rows + 2, WIDTH, CH)
    act_pad = jnp.pad(extended, ((0, 0), (0, 0), (1, 1), (0, 0)))
    cot_four = cotangent.reshape(frames, rows, WIDTH, CH)
    cot_flat = cot_four.reshape(-1, CH)
    output = jnp.zeros((frames * rows * WIDTH, CH), jnp.float32)
    blocks = []
    for step_t in range(3):
        for step_h in range(3):
            for step_w in range(3):
                offset = ((step_t * 3 + step_h) * 3 + step_w) * CH
                kernel = weight[offset : offset + CH]
                piece = act_pad[
                    step_t : step_t + frames, step_h : step_h + rows, step_w : step_w + WIDTH
                ].reshape(-1, CH)
                output = output + jnp.dot(piece, kernel, preferred_element_type=jnp.float32)
                blocks.append(
                    lax.dot_general(
                        piece,
                        cot_flat,
                        (((0,), (0,)), ((), ())),
                        preferred_element_type=jnp.float32,
                    )
                )
    spread = jnp.zeros((frames + 2, rows + 2, WIDTH + 2, CH), jnp.float32)
    for step_t in range(3):
        slab_weight = weight[step_t * 9 * CH : (step_t + 1) * 9 * CH]
        terms = lax.dot_general(
            cot_flat, slab_weight, (((1,), (1,)), ((), ())), preferred_element_type=jnp.float32
        )
        terms = terms.reshape(frames, rows, WIDTH, 9, CH)
        slab = jnp.zeros((frames, rows + 2, WIDTH + 2, CH), jnp.float32)
        for step_h in range(3):
            for step_w in range(3):
                slab = slab + jnp.pad(
                    terms[:, :, :, step_h * 3 + step_w],
                    ((0, 0), (step_h, 2 - step_h), (step_w, 2 - step_w), (0, 0)),
                )
        spread = spread + jnp.pad(slab, ((step_t, 2 - step_t), (0, 0), (0, 0), (0, 0)))
    inner = spread[:, :, 1 : WIDTH + 1]
    from_next = passed_along(inner[:, 0:1], "row", -1)
    from_prev = passed_along(inner[:, rows + 1 : rows + 2], "row", 1)
    center = inner[:, 1 : rows + 1]
    center = center.at[:, rows - 1 : rows].add(from_next)
    center = center.at[:, 0:1].add(from_prev)
    returned = passed_along(center[0:2], "tm", -1)
    grad_act = center[2:].at[frames - 2 :].add(returned).reshape(-1, CH)
    x_float = inputs.reshape(-1, CH).astype(jnp.float32)
    sigma = jax.nn.sigmoid(x_float)
    input_grad = (grad_act * sigma * (1.0 + x_float * (1.0 - sigma))).astype(jnp.bfloat16)
    local_filter = jnp.concatenate(blocks, 0).reshape(-1)
    frame_blocks = lax.axis_size("tm")
    row_blocks = lax.axis_size("row")
    scale = frames * frame_blocks * rows * row_blocks
    share = lax.psum_scatter(local_filter, ("tm", "row"), scatter_dimension=0, tiled=True)
    filter_grad = (share / scale).astype(jnp.bfloat16)
    shape = (frames, rows, WIDTH * CH)
    return (output.astype(jnp.bfloat16).reshape(shape), input_grad.reshape(shape), filter_grad)


def solution(mesh):
    placed = (P(("grp", "tm"), "row", None), P(), P(("grp", "tm"), "row", None))
    return jax.shard_map(
        on_device,
        mesh=mesh,
        in_specs=placed,
        out_specs=(
            P(("grp", "tm"), "row", None),
            P(("grp", "tm"), "row", None),
            P(("grp", "tm", "row")),
        ),
        check_vma=False,
    )
```

profile of v0, /device:TPU:31, one launch (start us, length us, event | category | flops | bytes accessed | tf_op | source)
XLA Modules:
  0.0 262.5 jit_solution(4734210250937015985)
XLA Ops:
  7.2 1.9 fusion.42
  10.3 1.6 slice_bitcast_fusion.8
  12.8 1.7 slice_bitcast_fusion.17
  18.2 1.3 pad_add_fusion.1
  20.2 1.3 collective-permute-start.4
  21.5 4.0 %collective-permute-start.3 = (f32[4,1,224,192]{2,3,0,1:T(8,128)S(1)}, f32[4,1,224,192]{2,3,0,1:T(8,128)S(1)}, u32[]{:S(2)}, u32[]{:S(2)}) collective-permute-start(f32[4,1,224,192]{2,3,0,1:T(8,128)S(1)} %get-tuple-element.90), channel_id=1, source_target_pairs={{1,0},{2,1},{3,2},{4,3},{5,4},{6,5},{7,6},{9,8},{10,9},{11,10},{12... | collective-permute-start | bytes 2064392 | tf_op jit(solution)/shard_map/ppermute | solution.py:13
  25.6 14.9 %collective-permute-done.4 = f32[4,1,224,192]{2,3,0,1:T(8,128)S(1)} collective-permute-done((f32[4,1,224,192]{2,3,0,1:T(8,128)S(1)}, f32[4,1,224,192]{2,3,0,1:T(8,128)S(1)}, u32[]{:S(2)}, u32[]{:S(2)}) %collective-permute-start.4) | collective-permute-done | bytes 688160 | tf_op jit(solution)/shard_map/ppermute | solution.py:13
  40.5 16.9 %collective-permute-done.3 = f32[4,1,224,192]{2,3,0,1:T(8,128)S(1)} collective-permute-done((f32[4,1,224,192]{2,3,0,1:T(8,128)S(1)}, f32[4,1,224,192]{2,3,0,1:T(8,128)S(1)}, u32[]{:S(2)}, u32[]{:S(2)}) %collective-permute-start.3) | collective-permute-done | bytes 688160 | tf_op jit(solution)/shard_map/ppermute | solution.py:13
  57.8 2.6 collective-permute-start.5
  60.3 1.3 collective-permute-done.5
  62.2 1.3 fusion.8
  63.6 1.3 collective-permute-start
  64.9 2.0 collective-permute-done
  67.2 4.1 %collective-permute-start.2 = (bf16[4,1,43008]{2,0,1:T(4,128)(2,1)S(1)}, bf16[4,1,43008]{2,0,1:T(4,128)(2,1)S(1)}, u32[]{:S(2)}, u32[]{:S(2)}) collective-permute-start(bf16[4,1,43008]{2,0,1:T(4,128)(2,1)S(1)} %pad_maximum_fusion.1), channel_id=1, source_target_pairs={{1,0},{2,1},{3,2},{4,3},{5,4},{6,5},{7,6},{9,8},{10,9},{11,10},{12... | collective-permute-start | bytes 1032200 | tf_op jit(solution)/shard_map/ppermute | solution.py:24
  71.4 1.3 collective-permute-start.1
  74.1 11.9 %collective-permute-done.2 = bf16[4,1,43008]{2,0,1:T(4,128)(2,1)S(1)} collective-permute-done((bf16[4,1,43008]{2,0,1:T(4,128)(2,1)S(1)}, bf16[4,1,43008]{2,0,1:T(4,128)(2,1)S(1)}, u32[]{:S(2)}, u32[]{:S(2)}) %collective-permute-start.2) | collective-permute-done | bytes 344096 | tf_op jit(solution)/shard_map/ppermute | solution.py:24
  86.6 1.8 reshape.236
  89.4 1.2 copy-done
  91.1 1.0 fusion.45
  92.3 1.0 fusion.46
  94.7 1.0 fusion.48
  97.1 1.0 fusion.50
  98.3 1.0 fusion.51
  100.7 1.0 fusion.53
  104.4 1.0 fusion.56
  105.6 1.0 fusion.57
  106.5 1.2 convolution_add_fusion.13
  108.7 1.1 convolution_add_fusion.12
  110.8 1.2 convolution_add_fusion.11
  112.9 1.1 convolution_add_fusion.10
  114.0 1.0 fusion.61
  115.0 1.2 convolution_add_fusion.9
  117.1 1.1 convolution_add_fusion.8
  118.2 1.0 fusion.63
  121.1 1.0 fusion.66
  125.8 6.1 %concatenate.17 = f32[5184,192]{0,1:T(8,128)} concatenate(f32[192,192]{0,1:T(8,128)S(1)} %fusion.44, f32[192,192]{0,1:T(8,128)S(1)} %copy-done.16, f32[192,192]{0,1:T(8,128)S(1)} %copy-done.17, f32[192,192]{0,1:T(8,128)S(1)} %copy-done.18, f32[192,192]{0,1:T(8,128)S(1)} %copy-done.19, f32[192,192]{0,1:T(8,128)} %fusion.49, f32[192,192]{0,1:T(8,128)} %fusion.50, ...), dimensions={0} | concatenate | bytes 7962624 | tf_op jit(solution)/shard_map/concatenate | solution.py:85
  131.9 5.7 %copy.59 = f32[5184,192]{1,0:T(8,128)} copy(f32[5184,192]{0,1:T(8,128)} %concatenate.17) | data formatting | bytes 7962624 | tf_op jit(solution)/shard_map/concatenate | solution.py:85
  137.6 6.6 %reshape.267 = f32[995328]{0:T(1024)} reshape(f32[5184,192]{1,0:T(8,128)} %copy.59) | data formatting | bytes 7962624 | tf_op jit(solution)/shard_map/reshape | solution.py:85
  144.2 1.2 convolution_add_fusion.7
  145.4 1.1 convolution_add_fusion.6
  146.5 1.2 convolution_add_fusion.5
  147.7 1.1 convolution_add_fusion.4
  148.8 1.2 convolution_add_fusion.3
  150.0 1.1 convolution_add_fusion.2
  151.1 1.2 convolution_add_fusion.1
  152.3 1.2 fusion
  154.6 99.4 %all-reduce.34.cloned.1.call-done = f32[995328]{0:T(1024)} async-done(((f32[995328]{0:T(1024)}), f32[995328]{0:T(1024)}) %all-reduce.34.cloned.1.call-update) | async-done | bytes 3981328
  254.0 1.7 fusion.9
  (102 shorter events, 28.8 us)
Async XLA Ops:
  7.2 2.2 copy-start.20
  7.2 246.8 %all-reduce.34.cloned.1.call-start = ((), (), s32[]{:S(2)}) async-start(), calls=%async_computation | async-start | bytes 7962624
  15.5 1.1 copy-start.13
  15.5 1.1 copy-start.14
  15.5 1.2 copy-start.15
  15.8 1.1 copy-start.1
  15.8 1.2 copy-start.2
  15.8 1.3 copy-start.3
  15.8 1.4 copy-start.4
  15.8 1.5 copy-start.5
  15.9 1.6 copy-start.6
  15.9 1.8 copy-start.7
  15.9 1.9 copy-start.8
  15.9 2.0 copy-start.9
  15.9 2.1 copy-start.10
  15.9 2.2 copy-start.11
  15.9 2.3 copy-start.12
  20.2 20.3 %collective-permute-start.4 = (f32[4,1,224,192]{2,3,0,1:T(8,128)S(1)}, f32[4,1,224,192]{2,3,0,1:T(8,128)S(1)}, u32[]{:S(2)}, u32[]{:S(2)}) collective-permute-start(f32[4,1,224,192]{2,3,0,1:T(8,128)S(1)} %get-tuple-element.91), channel_id=1, source_target_pairs={{0,1},{1,2},{2,3},{3,4},{4,5},{5,6},{6,7},{8,9},{9,10},{10,11},{11... | collective-permute-start | bytes 2064392 | tf_op jit(solution)/shard_map/ppermute | solution.py:13
  21.5 35.9 %collective-permute-start.3 = (f32[4,1,224,192]{2,3,0,1:T(8,128)S(1)}, f32[4,1,224,192]{2,3,0,1:T(8,128)S(1)}, u32[]{:S(2)}, u32[]{:S(2)}) collective-permute-start(f32[4,1,224,192]{2,3,0,1:T(8,128)S(1)} %get-tuple-element.90), channel_id=1, source_target_pairs={{1,0},{2,1},{3,2},{4,3},{5,4},{6,5},{7,6},{9,8},{10,9},{11,10},{12... | collective-permute-start | bytes 2064392 | tf_op jit(solution)/shard_map/ppermute | solution.py:13
  57.7 4.5 %copy-start.21 = (bf16[2,1,43008]{2,0,1:T(2,128)(2,1)S(1)}, bf16[2,1,43008]{2,0,1:T(2,128)(2,1)}, u32[]{:S(2)}) copy-start(bf16[2,1,43008]{2,0,1:T(2,128)(2,1)} %param.15) | copy-start | bytes 516100
  57.8 3.9 %collective-permute-start.5 = (f32[2,1,224,192]{2,3,0,1:T(8,128)S(1)}, f32[2,1,224,192]{2,3,0,1:T(8,128)S(1)}, u32[]{:S(2)}, u32[]{:S(2)}) collective-permute-start(f32[2,1,224,192]{2,3,0,1:T(8,128)S(1)} %slice.481), channel_id=1, source_target_pairs={{8,0},{9,1},{10,2},{11,3},{12,4},{13,5},{14,6},{15,7},{24,16},{25,... | collective-permute-start | bytes 1032200 | tf_op jit(solution)/shard_map/ppermute | solution.py:13
  61.7 11.2 %copy-start.22 = (u32[32]{0:T(128)S(1)}, u32[32]{0:T(128)}, u32[]{:S(2)}) copy-start(u32[32]{0:T(128)} %constant.175) | copy-start | bytes 388
  63.6 3.3 %collective-permute-start = (bf16[2,1,43008]{2,0,1:T(2,128)(2,1)S(1)}, bf16[2,1,43008]{2,0,1:T(2,128)(2,1)S(1)}, u32[]{:S(2)}, u32[]{:S(2)}) collective-permute-start(bf16[2,1,43008]{2,0,1:T(2,128)(2,1)S(1)} %get-tuple-element.123), channel_id=1, source_target_pairs={{0,8},{1,9},{2,10},{3,11},{4,12},{5,13},{6,14},{7,15},{16,24},{17,... | collective-permute-start | bytes 516104 | tf_op jit(solution)/shard_map/ppermute | solution.py:13
  67.2 18.8 %collective-permute-start.2 = (bf16[4,1,43008]{2,0,1:T(4,128)(2,1)S(1)}, bf16[4,1,43008]{2,0,1:T(4,128)(2,1)S(1)}, u32[]{:S(2)}, u32[]{:S(2)}) collective-permute-start(bf16[4,1,43008]{2,0,1:T(4,128)(2,1)S(1)} %pad_maximum_fusion.1), channel_id=1, source_target_pairs={{1,0},{2,1},{3,2},{4,3},{5,4},{6,5},{7,6},{9,8},{10,9},{11,10},{12... | collective-permute-start | bytes 1032200 | tf_op jit(solution)/shard_map/ppermute | solution.py:24
  71.4 14.7 %collective-permute-start.1 = (bf16[4,1,43008]{2,0,1:T(4,128)(2,1)S(1)}, bf16[4,1,43008]{2,0,1:T(4,128)(2,1)S(1)}, u32[]{:S(2)}, u32[]{:S(2)}) collective-permute-start(bf16[4,1,43008]{2,0,1:T(4,128)(2,1)S(1)} %pad_maximum_fusion.1), channel_id=1, source_target_pairs={{0,1},{1,2},{2,3},{3,4},{4,5},{5,6},{6,7},{8,9},{9,10},{10,11},{11... | collective-permute-start | bytes 1032200 | tf_op jit(solution)/shard_map/ppermute | solution.py:23
  89.0 1.6 copy-start
  120.1 5.7 %copy-start.16 = (f32[192,192]{0,1:T(8,128)S(1)}, f32[192,192]{0,1:T(8,128)}, u32[]{:S(2)}) copy-start(f32[192,192]{0,1:T(8,128)} %fusion.45) | copy-start | bytes 442372
  120.1 5.7 %copy-start.17 = (f32[192,192]{0,1:T(8,128)S(1)}, f32[192,192]{0,1:T(8,128)}, u32[]{:S(2)}) copy-start(f32[192,192]{0,1:T(8,128)} %fusion.46) | copy-start | bytes 442372
  120.1 5.7 %copy-start.18 = (f32[192,192]{0,1:T(8,128)S(1)}, f32[192,192]{0,1:T(8,128)}, u32[]{:S(2)}) copy-start(f32[192,192]{0,1:T(8,128)} %fusion.47) | copy-start | bytes 442372
  120.1 5.7 %copy-start.19 = (f32[192,192]{0,1:T(8,128)S(1)}, f32[192,192]{0,1:T(8,128)}, u32[]{:S(2)}) copy-start(f32[192,192]{0,1:T(8,128)} %fusion.48) | copy-start | bytes 442372
Sparse Core Ops, SparseCore 0:
  144.3 109.5 all-reduce.33
where the time goes:
time: 268 us; the launch traced here: 263 us
  waiting for transfers between devices  146 us (54%)
  matrix products  46.2 us (17%)
  local copies, waits for them, and re-layouts  33.4 us (12%)
  between operations  15.3 us (6%)
  starting transfers between devices  14.6 us (5%)
  other arithmetic  6.6 us (2%)
    unnamed x2, waiting for transfers between devices  99.4 us
    ppermute x4, waiting for transfers between devices, passed_along(): return lax.ppermute(array, axis, pairs)  35.1 us
    dot_general x27, matrix products, on_device(): lax.dot_general(piece, cot_flat, (((0,), (0,)), ((), ())), preferred_elem...  25.1 us
    dot_general x27, matrix products, on_device(): output = output + jnp.dot(piece, kernel, preferred_element_type=jnp.float32)  19.2 us
    ppermute x1, waiting for transfers between devices, with_halo(): after = lax.ppermute(first, axis, down)  11.9 us
    concatenate x2, local copies, waits for them, and re-layouts, on_device(): local_filter = jnp.concatenate(blocks, 0).reshape(-1)  11.7 us
    ppermute x4, starting transfers between devices, passed_along(): return lax.ppermute(array, axis, pairs)  9.16 us
    reshape x1, local copies, waits for them, and re-layouts, on_device(): local_filter = jnp.concatenate(blocks, 0).reshape(-1)  6.59 us
  transfers between devices with their start and end apart: 7, of which 6 were waited for; matrix products, arithmetic and copies ran while one was open for 4% of the time, Pallas kernels for 0%

commit v1 on v0

--- a/solution.py
+++ b/solution.py
@@ -1,10 +1,367 @@
+import functools
+
 import jax
 import jax.numpy as jnp
 from jax import lax
+from jax.experimental import pallas as pl
+from jax.experimental.pallas import tpu as pltpu
 from jax.sharding import PartitionSpec as P
 
 CH = 192
 WIDTH = 224
+TAPS = 27
+BLOCK = 2 * WIDTH
+
+
+def fused_kernel(
+    pairs, chunk, scale, x_ref, w_ref, c_ref, out_ref, ig_ref, fg_ref,
+    act, cot, shifted, filt, outgoing, incoming, fwd, bwd, pad,
+    send_sem, recv_sem, piece_send, piece_recv,
+):
+    f32, bf16 = jnp.float32, jnp.bfloat16
+    grp, tm, row = lax.axis_index("grp"), lax.axis_index("tm"), lax.axis_index("row")
+    rows = 2 * pairs
+    pair, side = row // 2, row % 2
+    own = 1 + side
+    window = (side + pair) % 2
+
+    def device(t, r):
+        return (grp, t, r)
+
+    barrier = pltpu.get_barrier_semaphore()
+    me = tm * rows + row
+
+    @pl.loop(1, 2 * rows)
+    def _(step):
+        other = lax.rem(me + step, 2 * rows)
+        pl.semaphore_signal(
+            barrier, inc=1, device_id=device(other // rows, other % rows),
+            device_id_type=pl.DeviceIdType.MESH,
+        )
+
+    def act_at(slot, half):
+        return act.at[slot, pl.ds(pl.multiple_of((half + 1) * BLOCK, 16), BLOCK), :]
+
+    def cot_at(slot, half):
+        return cot.at[slot, pl.ds(pl.multiple_of(half * BLOCK, 16), BLOCK), :]
+
+    at = (act_at, cot_at)
+
+    def move(array, src_slot, dst_slot, half, lane, target):
+        return pltpu.make_async_remote_copy(
+            src_ref=at[array](src_slot, half),
+            dst_ref=at[array](dst_slot, half),
+            send_sem=send_sem.at[lane],
+            recv_sem=recv_sem.at[array, dst_slot, half],
+            device_id=target,
+            device_id_type=pl.DeviceIdType.MESH,
+        )
+
+    def arrived(array, slot, half):
+        move(array, slot, slot, half, 0, sibling).wait_recv()
+
+    sibling = device(1 - tm, row)
+    partner = device(tm, 2 * pair + 1 - side)
+    outer_pair = pair + 2 * side - 1
+    has_outer = jnp.logical_and(outer_pair >= 0, outer_pair < pairs)
+    outer_same = device(tm, 2 * outer_pair + side)
+    outer_cross = device(tm, 2 * outer_pair + 1 - side)
+    outer_slot = 3 * (1 - side)
+    cot_slot = 3 * side
+    has_before, has_after = pair > 0, pair < pairs - 1
+
+    x = x_ref[...].astype(f32)
+    act[own, pl.ds(pl.multiple_of((tm + 1) * BLOCK, 16), BLOCK), :] = (
+        x * (1.0 / (1.0 + jnp.exp(-x)))
+    ).astype(bf16)
+    cot[own, pl.ds(pl.multiple_of(tm * BLOCK, 16), BLOCK), :] = c_ref[...]
+    pl.semaphore_wait(barrier, 2 * rows - 1)
+
+    straight = [
+        move(0, own, own, tm, 2, partner),
+        move(1, own, own, tm, 3, partner),
+        move(0, own, own, tm, 0, sibling),
+        move(1, own, own, tm, 1, sibling),
+    ]
+    outward = [
+        move(0, own, outer_slot, tm, 4, outer_cross),
+        move(1, own, outer_slot, tm, 5, outer_cross),
+        move(0, own, outer_slot, tm, 6, outer_same),
+    ]
+
+    @pl.when(has_outer)
+    def _():
+        for copy in outward:
+            copy.start()
+
+    for copy in straight:
+        copy.start()
+
+    for slot in range(4):
+        act[slot, 0:BLOCK, :] = jnp.zeros((BLOCK, CH), bf16)
+        cot[slot, 2 * BLOCK : 3 * BLOCK, :] = jnp.zeros((BLOCK, CH), bf16)
+
+    for slot, present in ((0, has_before), (3, has_after)):
+
+        @pl.when(jnp.logical_not(present))
+        def _():
+            act[slot, BLOCK : 3 * BLOCK, :] = jnp.zeros((2 * BLOCK, CH), bf16)
+            cot[slot, 0 : 2 * BLOCK, :] = jnp.zeros((2 * BLOCK, CH), bf16)
+
+    pad[0:8, :] = jnp.zeros((8, CH), f32)
+    pad[WIDTH + 8 : WIDTH + 16, :] = jnp.zeros((8, CH), f32)
+
+    def tap_weight(step_t, step_h, step_w):
+        offset = ((step_t * 3 + step_h) * 3 + step_w) * CH
+        return w_ref[pl.ds(pl.multiple_of(offset, 16), CH), :]
+
+    def convolve(step_h, first):
+        @pl.loop(0, 3)
+        def _(step_t):
+            a = act[side + step_h, pl.ds(pl.multiple_of((2 * tm + step_t) * WIDTH, 16), BLOCK), :]
+            c = cot[
+                side + 2 - step_h,
+                pl.ds(pl.multiple_of((2 * tm + 2 - step_t) * WIDTH, 16), BLOCK),
+                :,
+            ]
+            for step_w in range(3):
+                kernel = tap_weight(step_t, step_h, step_w)
+                y = jnp.dot(a, kernel, preferred_element_type=f32)
+                z = lax.dot_general(
+                    c, kernel, (((1,), (1,)), ((), ())), preferred_element_type=f32
+                )
+                if first:
+
+                    @pl.when(step_t == 0)
+                    def _():
+                        fwd[step_w] = y
+                        bwd[step_w] = z
+
+                    @pl.when(step_t > 0)
+                    def _():
+                        fwd[step_w] += y
+                        bwd[step_w] += z
+                else:
+                    fwd[step_w] += y
+                    bwd[step_w] += z
+
+    other_slot = 2 - side
+    arrived(0, own, 1 - tm)
+    arrived(1, own, 1 - tm)
+    convolve(1, True)
+
+    onward = [move(0, other_slot, other_slot, tm, 7, sibling), move(1, other_slot, other_slot, tm, 8, sibling)]
+    arrived(0, other_slot, tm)
+    onward[0].start()
+    arrived(1, other_slot, tm)
+    onward[1].start()
+    before = move(0, 0, 0, tm, 9, sibling)
+    after = move(0, 3, 3, tm, 10, sibling)
+    edge = move(1, cot_slot, cot_slot, tm, 11, sibling)
+
+    @pl.when(has_before)
+    def _():
+        arrived(0, 0, tm)
+        before.start()
+
+    @pl.when(has_after)
+    def _():
+        arrived(0, 3, tm)
+        after.start()
+
+    @pl.when(has_outer_cot(pair, side, pairs))
+    def _():
+        arrived(1, cot_slot, tm)
+        edge.start()
+
+    arrived(0, other_slot, 1 - tm)
+    arrived(1, other_slot, 1 - tm)
+
+    for h in range(2):
+
+        @pl.loop(0, 4)
+        def _(frame):
+            rows_of = pl.ds(pl.multiple_of(frame * WIDTH, 16), WIDTH)
+            value = cot[1 + h, rows_of, :]
+            pad[8 : WIDTH + 8, :] = value.astype(f32)
+            shifted[0, h, rows_of, :] = pad[9 : WIDTH + 9, :].astype(bf16)
+            shifted[1, h, rows_of, :] = value
+            shifted[2, h, rows_of, :] = pad[7 : WIDTH + 7, :].astype(bf16)
+
+    @pl.when(has_before)
+    def _():
+        arrived(0, 0, 1 - tm)
+
+    @pl.when(has_after)
+    def _():
+        arrived(0, 3, 1 - tm)
+
+    quarter = 2 * tm + window
+    per_window = pairs * chunk
+    held = filt.shape[0] // CH
+    starts = [min(q * per_window // CH, TAPS - held) for q in range(4)]
+    first_tap = jnp.int32(starts[0])
+    for q in range(1, 4):
+        first_tap = jnp.where(quarter == q, jnp.int32(starts[q]), first_tap)
+
+    @pl.loop(0, held)
+    def _(n):
+        tap = first_tap + n
+        step_t, step_h, step_w = tap // 9, (tap // 3) % 3, tap % 3
+        span = pl.ds(pl.multiple_of(step_t * WIDTH, 16), 4 * WIDTH)
+        total = None
+        for h in range(2):
+            term = lax.dot_general(
+                act[h + step_h, span, :],
+                shifted[step_w, h],
+                (((0,), (0,)), ((), ())),
+                preferred_element_type=f32,
+            )
+            total = term if total is None else total + term
+        filt[pl.ds(pl.multiple_of(n * CH, 16), CH), :] = total
+
+    for q in range(4):
+
+        @pl.when(quarter == q)
+        def _():
+            base = q * per_window - starts[q] * CH
+            for i in range(pairs):
+                outgoing[i] = filt[base + i * chunk : base + (i + 1) * chunk, :].astype(bf16)
+
+    pieces = []
+    for i in range(pairs):
+        owner = window * pairs + i
+        piece = pltpu.make_async_remote_copy(
+            src_ref=outgoing.at[i],
+            dst_ref=incoming.at[pair],
+            send_sem=piece_send.at[i],
+            recv_sem=piece_recv.at[pair],
+            device_id=device(tm, owner),
+            device_id_type=pl.DeviceIdType.MESH,
+        )
+        pieces.append((owner, piece))
+
+        @pl.when(owner != row)
+        def _():
+            piece.start()
+
+        @pl.when(owner == row)
+        def _():
+            incoming[pair] = outgoing[i]
+
+    @pl.when(has_outer_cot(pair, side, pairs))
+    def _():
+        arrived(1, cot_slot, 1 - tm)
+
+    convolve(0, False)
+    convolve(2, False)
+
+    for frame in range(2):
+        span = pl.ds(frame * WIDTH, WIDTH)
+        inner = pl.ds(8, WIDTH)
+        pad[inner, :] = fwd[0, span, :]
+        value = fwd[1, span, :] + pad[7 : WIDTH + 7, :]
+        pad[inner, :] = fwd[2, span, :]
+        value = value + pad[9 : WIDTH + 9, :]
+        out_ref[span, :] = value.astype(bf16)
+        pad[inner, :] = bwd[0, span, :]
+        value = bwd[1, span, :] + pad[9 : WIDTH + 9, :]
+        pad[inner, :] = bwd[2, span, :]
+        value = value + pad[7 : WIDTH + 7, :]
+        x = x_ref[span, :].astype(f32)
+        sigma = 1.0 / (1.0 + jnp.exp(-x))
+        ig_ref[span, :] = (value * sigma * (1.0 + x * (1.0 - sigma))).astype(bf16)
+
+    for source in range(pairs):
+        from_row = 2 * source + (row // pairs + source) % 2
+
+        @pl.when(from_row != row)
+        def _():
+            pltpu.make_async_remote_copy(
+                src_ref=outgoing.at[0],
+                dst_ref=incoming.at[source],
+                send_sem=piece_send.at[0],
+                recv_sem=piece_recv.at[source],
+                device_id=sibling,
+                device_id_type=pl.DeviceIdType.MESH,
+            ).wait_recv()
+
+    total = incoming[0].astype(f32)
+    for source in range(1, pairs):
+        total = total + incoming[source].astype(f32)
+    fg_ref[...] = (total / scale).astype(bf16)
+
+    for copy in straight + onward:
+        copy.wait_send()
+
+    @pl.when(has_outer)
+    def _():
+        for copy in outward:
+            copy.wait_send()
+        edge.wait_send()
+
+    @pl.when(has_before)
+    def _():
+        before.wait_send()
+
+    @pl.when(has_after)
+    def _():
+        after.wait_send()
+
+    for owner, piece in pieces:
+
+        @pl.when(owner != row)
+        def _():
+            piece.wait_send()
+
+
+def has_outer_cot(pair, side, pairs):
+    outer = pair + 2 * side - 1
+    return jnp.logical_and(outer >= 0, outer < pairs)
+
+
+def fused(inputs, weight, cotangent):
+    frames, rows = inputs.shape[:2]
+    tm_size, row_size = lax.axis_size("tm"), lax.axis_size("row")
+    pairs = row_size // 2
+    chunk = TAPS * CH // (2 * row_size)
+    scale = frames * tm_size * rows * row_size
+    quarter_rows = pairs * chunk
+    held = max(
+        -(-(q + 1) * quarter_rows // CH) - q * quarter_rows // CH for q in range(4)
+    )
+    vmem = pl.BlockSpec(memory_space=pltpu.VMEM)
+    bf16, f32 = jnp.bfloat16, jnp.float32
+    out, ig, fg = pl.pallas_call(
+        functools.partial(fused_kernel, pairs, chunk, float(scale)),
+        out_shape=(
+            jax.ShapeDtypeStruct((BLOCK, CH), bf16),
+            jax.ShapeDtypeStruct((BLOCK, CH), bf16),
+            jax.ShapeDtypeStruct((chunk, CH), bf16),
+        ),
+        in_specs=[vmem] * 3,
+        out_specs=(vmem, vmem, vmem),
+        scratch_shapes=[
+            pltpu.VMEM((4, 3 * BLOCK, CH), bf16),
+            pltpu.VMEM((4, 3 * BLOCK, CH), bf16),
+            pltpu.VMEM((3, 2, 2 * BLOCK, CH), bf16),
+            pltpu.VMEM((held * CH, CH), f32),
+            pltpu.VMEM((pairs, chunk, CH), bf16),
+            pltpu.VMEM((pairs, chunk, CH), bf16),
+            pltpu.VMEM((3, BLOCK, CH), f32),
+            pltpu.VMEM((3, BLOCK, CH), f32),
+            pltpu.VMEM((WIDTH + 16, CH), f32),
+            pltpu.SemaphoreType.DMA((12,)),
+            pltpu.SemaphoreType.DMA((2, 4, 2)),
+            pltpu.SemaphoreType.DMA((pairs,)),
+            pltpu.SemaphoreType.DMA((pairs,)),
+        ],
+        compiler_params=pltpu.CompilerParams(
+            collective_id=0, has_side_effects=True, vmem_limit_bytes=48 * 1024 * 1024
+        ),
+    )(inputs.reshape(BLOCK, CH), weight, cotangent.reshape(BLOCK, CH))
+    shape = (frames, rows, WIDTH * CH)
+    return out.reshape(shape), ig.reshape(shape), fg.reshape(-1)
 
 
 def passed_along(array, axis, by):
@@ -92,10 +449,18 @@
     return (output.astype(jnp.bfloat16).reshape(shape), input_grad.reshape(shape), filter_grad)
 
 
+def either(mesh, inputs, weight, cotangent):
+    size = mesh.shape["row"]
+    quads = mesh.shape["tm"] == 2 and size % 2 == 0 and TAPS * CH % (2 * size) == 0
+    if quads and inputs.shape[:2] == (2, 1):
+        return fused(inputs, weight, cotangent)
+    return on_device(inputs, weight, cotangent)
+
+
 def solution(mesh):
     placed = (P(("grp", "tm"), "row", None), P(), P(("grp", "tm"), "row", None))
     return jax.shard_map(
-        on_device,
+        functools.partial(either, mesh),
         mesh=mesh,
         in_specs=placed,
         out_specs=(

time: 268 us -> 60.3 us (0.22); the launches traced: 263 us -> 60.1 us
  waiting for transfers between devices: 146 us -> 0 us
  Pallas kernels: 0 us -> 48.8 us
  matrix products: 46.2 us -> 0 us
  local copies, waits for them, and re-layouts: 33.4 us -> 10.6 us
  between operations: 15.3 us -> 0.67 us
  starting transfers between devices: 14.6 us -> 0 us
  other arithmetic: 6.6 us -> 0 us
    unnamed x2 -> x0, waiting for transfers between devices: 99.4 us -> none
    pallas_call x0 -> x1, Pallas kernels: none -> 48.8 us  [fused(): pl.pallas_call(functools.partial(fused_kernel, pairs, chunk, float(scale)...]
    ppermute x6 -> x0, waiting for transfers between devices: 47 us -> none  [the longest x4 35.1 us: passed_along(): return lax.ppermute(array, axis, pairs)]
    dot_general x57 -> x0, matrix products: 46.2 us -> none  [the longest x27 25.1 us: on_device(): lax.dot_general(piece, cot_flat, (((0,), (0,)), ((), ())), preferred_elem...]
    ppermute x6 -> x0, starting transfers between devices: 14.6 us -> none  [the longest x4 9.16 us: passed_along(): return lax.ppermute(array, axis, pairs)]
    concatenate x2 -> x0, local copies, waits for them, and re-layouts: 11.7 us -> none  [on_device(): local_filter = jnp.concatenate(blocks, 0).reshape(-1)]
    slice x9 -> x0, local copies, waits for them, and re-layouts: 4.25 us -> none  [the longest x4 2.78 us: on_device(): slab_weight = weight[step_t * 9 * CH:(step_t + 1) * 9 * CH]]
    reshape x4 -> x5, local copies, waits for them, and re-layouts: 9.67 us -> 6.05 us  [the longest x3 3.73 us: fused(): return (out.reshape(shape), ig.reshape(shape), fg.reshape(-1))]
  transfers between devices with their start and end apart: 7 -> 0, of which waited for: 6 -> 0; matrix products, arithmetic and copies ran while one was open for 4% -> 0% of each run, Pallas kernels for 0% -> 0%
where the time goes in v1:
time: 60.3 us; the launch traced here: 60.1 us
  Pallas kernels  48.8 us (81%)
  local copies, waits for them, and re-layouts  10.6 us (18%)
  between operations  0.67 us (1%)
    pallas_call x1, Pallas kernels, fused(): pl.pallas_call(functools.partial(fused_kernel, pairs, chunk, float(scale)...  48.8 us
    unnamed x3, local copies, waits for them, and re-layouts  4.53 us
    reshape x3, local copies, waits for them, and re-layouts, fused(): return (out.reshape(shape), ig.reshape(shape), fg.reshape(-1))  3.73 us

profile of v1, /device:TPU:31, one launch (start us, length us, event | category | flops | bytes accessed | tf_op | source)
XLA Modules:
  0.0 60.1 jit_solution(6153979443860238246)
XLA Ops:
  0.6 1.2 %reshape.21.x_ref = bf16[448,192]{1,0:T(8,128)(2,1)S(1)} reshape(bf16[2,1,43008]{2,0,1:T(2,128)(2,1)} %param.3) | data formatting | bytes 344064 | tf_op jit(solution)/shard_map/reshape | solution.py:362
  1.8 1.2 %reshape.22.c_ref = bf16[448,192]{1,0:T(8,128)(2,1)S(1)} reshape(bf16[2,1,43008]{2,0,1:T(2,128)(2,1)} %param.5) | data formatting | bytes 344064 | tf_op jit(solution)/shard_map/reshape | solution.py:362
  3.0 3.9 %copy.7.w_ref = bf16[5184,192]{1,0:T(8,128)(2,1)S(1)} copy(bf16[5184,192]{0,1:T(8,128)(2,1)} %param.4) | data formatting | bytes 3981312 | tf_op args[1]
  6.8 48.8 %shard_map.58 = (bf16[448,192]{1,0:T(8,128)(2,1)S(1)}, bf16[448,192]{1,0:T(8,128)(2,1)S(1)}, bf16[324,192]{1,0:T(8,128)(2,1)S(1)}) custom-call(bf16[448,192]{1,0:T(8,128)(2,1)S(1)} %reshape.21.x_ref, bf16[5184,192]{1,0:T(8,128)(2,1)S(1)} %copy.7.w_ref, bf16[448,192]{1,0:T(8,128)(2,1)S(1)} %reshape.22.c_ref), custom_call_target="tpu_custom_call" | custom-call | tf_op jit(solution)/shard_map/pallas_call | solution.py:335
  55.7 0.0 copy-start
  55.7 0.7 %copy-done = bf16[448,192]{1,0:T(8,128)(2,1)} copy-done((bf16[448,192]{1,0:T(8,128)(2,1)}, bf16[448,192]{1,0:T(8,128)(2,1)S(1)}, u32[]{:S(2)}) %copy-start) | copy-done | bytes 172056
  56.4 1.9 %reshape.23 = bf16[2,1,43008]{2,0,1:T(2,128)(2,1)} reshape(bf16[448,192]{1,0:T(8,128)(2,1)} %copy-done) | data formatting | bytes 344064 | tf_op jit(solution)/shard_map/reshape | solution.py:364
  58.3 0.9 %reshape.25 = bf16[62208]{0:T(1024)(128)(2,1)} reshape(bf16[324,192]{1,0:T(8,128)(2,1)S(1)} %get-tuple-element.8) | data formatting | bytes 248832 | tf_op jit(solution)/shard_map/reshape | solution.py:364
  59.1 1.0 %reshape.24 = bf16[2,1,43008]{2,0,1:T(2,128)(2,1)} reshape(bf16[448,192]{1,0:T(8,128)(2,1)S(1)} %get-tuple-element.7) | data formatting | bytes 344064 | tf_op jit(solution)/shard_map/reshape | solution.py:364
Async XLA Ops:
  55.7 0.7 %copy-start = (bf16[448,192]{1,0:T(8,128)(2,1)}, bf16[448,192]{1,0:T(8,128)(2,1)S(1)}, u32[]{:S(2)}) copy-start(bf16[448,192]{1,0:T(8,128)(2,1)S(1)} %get-tuple-element.6) | copy-start | bytes 516100

commit v2 on v1

--- a/solution.py
+++ b/solution.py
@@ -11,12 +11,13 @@
 WIDTH = 224
 TAPS = 27
 BLOCK = 2 * WIDTH
+PACKED = 3 * WIDTH
 
 
 def fused_kernel(
     pairs, chunk, scale, x_ref, w_ref, c_ref, out_ref, ig_ref, fg_ref,
-    act, cot, shifted, filt, outgoing, incoming, fwd, bwd, pad,
-    send_sem, recv_sem, piece_send, piece_recv,
+    act, cot, packed, weight_in, taps, shifted, filt, outgoing, incoming, fwd, bwd, pad,
+    weight_sem, send_sem, recv_sem, piece_send, piece_recv,
 ):
     f32, bf16 = jnp.float32, jnp.bfloat16
     grp, tm, row = lax.axis_index("grp"), lax.axis_index("tm"), lax.axis_index("row")
@@ -28,6 +29,9 @@
     def device(t, r):
         return (grp, t, r)
 
+    fetch = pltpu.make_async_copy(w_ref, weight_in, weight_sem)
+    fetch.start()
+
     barrier = pltpu.get_barrier_semaphore()
     me = tm * rows + row
 
@@ -39,18 +43,28 @@
             device_id_type=pl.DeviceIdType.MESH,
         )
 
-    def act_at(slot, half):
-        return act.at[slot, pl.ds(pl.multiple_of((half + 1) * BLOCK, 16), BLOCK), :]
-
-    def cot_at(slot, half):
-        return cot.at[slot, pl.ds(pl.multiple_of(half * BLOCK, 16), BLOCK), :]
-
-    at = (act_at, cot_at)
+    def half_of(array, slot, half):
+        if array == 0:
+            return act, pl.multiple_of((half + 1) * BLOCK, 16)
+        return cot, pl.multiple_of(half * BLOCK, 16)
+
+    def pack(array, slot, half, value):
+        packed[array, slot, half, 0:BLOCK, :] = value[:, 0:128]
+        packed[array, slot, half, BLOCK:PACKED, :] = jnp.concatenate(
+            [value[0:WIDTH, 128:CH], value[WIDTH:BLOCK, 128:CH]], axis=1
+        )
+
+    def unpack(array, slot, half):
+        ref, base = half_of(array, slot, half)
+        ref[slot, pl.ds(base, BLOCK), 0:128] = packed[array, slot, half, 0:BLOCK, :]
+        high = packed[array, slot, half, BLOCK:PACKED, :]
+        ref[slot, pl.ds(base, WIDTH), 128:CH] = high[:, 0:64]
+        ref[slot, pl.ds(pl.multiple_of(base + WIDTH, 16), WIDTH), 128:CH] = high[:, 64:128]
 
     def move(array, src_slot, dst_slot, half, lane, target):
         return pltpu.make_async_remote_copy(
-            src_ref=at[array](src_slot, half),
-            dst_ref=at[array](dst_slot, half),
+            src_ref=packed.at[array, src_slot, half],
+            dst_ref=packed.at[array, dst_slot, half],
             send_sem=send_sem.at[lane],
             recv_sem=recv_sem.at[array, dst_slot, half],
             device_id=target,
@@ -71,10 +85,12 @@
     has_before, has_after = pair > 0, pair < pairs - 1
 
     x = x_ref[...].astype(f32)
-    act[own, pl.ds(pl.multiple_of((tm + 1) * BLOCK, 16), BLOCK), :] = (
-        x * (1.0 / (1.0 + jnp.exp(-x)))
-    ).astype(bf16)
-    cot[own, pl.ds(pl.multiple_of(tm * BLOCK, 16), BLOCK), :] = c_ref[...]
+    value = (x * (1.0 / (1.0 + jnp.exp(-x)))).astype(bf16)
+    act[own, pl.ds(pl.multiple_of((tm + 1) * BLOCK, 16), BLOCK), :] = value
+    pack(0, own, tm, value)
+    value = c_ref[...]
+    cot[own, pl.ds(pl.multiple_of(tm * BLOCK, 16), BLOCK), :] = value
+    pack(1, own, tm, value)
     pl.semaphore_wait(barrier, 2 * rows - 1)
 
     straight = [
@@ -85,16 +101,18 @@
     ]
     outward = [
         move(0, own, outer_slot, tm, 4, outer_cross),
+        move(0, own, outer_slot, tm, 6, outer_same),
         move(1, own, outer_slot, tm, 5, outer_cross),
-        move(0, own, outer_slot, tm, 6, outer_same),
     ]
+    for copy in straight[:2]:
+        copy.start()
 
     @pl.when(has_outer)
     def _():
-        for copy in outward:
+        for copy in outward[:2]:
             copy.start()
 
-    for copy in straight:
+    for copy in straight[2:]:
         copy.start()
 
     for slot in range(4):
@@ -111,24 +129,28 @@
     pad[0:8, :] = jnp.zeros((8, CH), f32)
     pad[WIDTH + 8 : WIDTH + 16, :] = jnp.zeros((8, CH), f32)
 
-    def tap_weight(step_t, step_h, step_w):
-        offset = ((step_t * 3 + step_h) * 3 + step_w) * CH
-        return w_ref[pl.ds(pl.multiple_of(offset, 16), CH), :]
-
-    def convolve(step_h, first):
+    fetch.wait()
+    for tap in range(TAPS):
+        taps[tap] = weight_in[:, tap * CH : (tap + 1) * CH]
+
+    def convolve(act_h, cot_h, first):
         @pl.loop(0, 3)
         def _(step_t):
-            a = act[side + step_h, pl.ds(pl.multiple_of((2 * tm + step_t) * WIDTH, 16), BLOCK), :]
+            a = act[side + act_h, pl.ds(pl.multiple_of((2 * tm + step_t) * WIDTH, 16), BLOCK), :]
             c = cot[
-                side + 2 - step_h,
+                side + 2 - cot_h,
                 pl.ds(pl.multiple_of((2 * tm + 2 - step_t) * WIDTH, 16), BLOCK),
                 :,
             ]
             for step_w in range(3):
-                kernel = tap_weight(step_t, step_h, step_w)
-                y = jnp.dot(a, kernel, preferred_element_type=f32)
-                z = lax.dot_general(
-                    c, kernel, (((1,), (1,)), ((), ())), preferred_element_type=f32
+                y = lax.dot_general(
+                    a,
+                    taps[(step_t * 3 + act_h) * 3 + step_w],
+                    (((1,), (1,)), ((), ())),
+                    preferred_element_type=f32,
+                )
+                z = jnp.dot(
+                    c, taps[(step_t * 3 + cot_h) * 3 + step_w], preferred_element_type=f32
                 )
                 if first:
 
@@ -145,40 +167,7 @@
                     fwd[step_w] += y
                     bwd[step_w] += z
 
-    other_slot = 2 - side
-    arrived(0, own, 1 - tm)
-    arrived(1, own, 1 - tm)
-    convolve(1, True)
-
-    onward = [move(0, other_slot, other_slot, tm, 7, sibling), move(1, other_slot, other_slot, tm, 8, sibling)]
-    arrived(0, other_slot, tm)
-    onward[0].start()
-    arrived(1, other_slot, tm)
-    onward[1].start()
-    before = move(0, 0, 0, tm, 9, sibling)
-    after = move(0, 3, 3, tm, 10, sibling)
-    edge = move(1, cot_slot, cot_slot, tm, 11, sibling)
-
-    @pl.when(has_before)
-    def _():
-        arrived(0, 0, tm)
-        before.start()
-
-    @pl.when(has_after)
-    def _():
-        arrived(0, 3, tm)
-        after.start()
-
-    @pl.when(has_outer_cot(pair, side, pairs))
-    def _():
-        arrived(1, cot_slot, tm)
-        edge.start()
-
-    arrived(0, other_slot, 1 - tm)
-    arrived(1, other_slot, 1 - tm)
-
-    for h in range(2):
-
+    def shift(h):
         @pl.loop(0, 4)
         def _(frame):
             rows_of = pl.ds(pl.multiple_of(frame * WIDTH, 16), WIDTH)
@@ -188,13 +177,32 @@
             shifted[1, h, rows_of, :] = value
             shifted[2, h, rows_of, :] = pad[7 : WIDTH + 7, :].astype(bf16)
 
-    @pl.when(has_before)
-    def _():
-        arrived(0, 0, 1 - tm)
-
-    @pl.when(has_after)
-    def _():
-        arrived(0, 3, 1 - tm)
+    other_slot = 2 - side
+    arrived(0, own, 1 - tm)
+    unpack(0, own, 1 - tm)
+    arrived(1, own, 1 - tm)
+    unpack(1, own, 1 - tm)
+    convolve(1, 1, True)
+    shift(side)
+
+    onward = [move(0, other_slot, other_slot, tm, 7, sibling), move(1, other_slot, other_slot, tm, 8, sibling)]
+    before = move(0, 0, 0, tm, 9, sibling)
+    after = move(0, 3, 3, tm, 10, sibling)
+    edge = move(1, cot_slot, cot_slot, tm, 11, sibling)
+    for array in range(2):
+        arrived(array, other_slot, tm)
+        onward[array].start()
+
+    @pl.when(has_outer)
+    def _():
+        outward[2].start()
+
+    for array in range(2):
+        unpack(array, other_slot, tm)
+    for array in range(2):
+        arrived(array, other_slot, 1 - tm)
+        unpack(array, other_slot, 1 - tm)
+    shift(1 - side)
 
     quarter = 2 * tm + window
     per_window = pairs * chunk
@@ -204,29 +212,75 @@
     for q in range(1, 4):
         first_tap = jnp.where(quarter == q, jnp.int32(starts[q]), first_tap)
 
-    @pl.loop(0, held)
-    def _(n):
+    def filter_term(n, h, slot):
         tap = first_tap + n
-        step_t, step_h, step_w = tap // 9, (tap // 3) % 3, tap % 3
-        span = pl.ds(pl.multiple_of(step_t * WIDTH, 16), 4 * WIDTH)
-        total = None
-        for h in range(2):
-            term = lax.dot_general(
-                act[h + step_h, span, :],
-                shifted[step_w, h],
-                (((0,), (0,)), ((), ())),
-                preferred_element_type=f32,
-            )
-            total = term if total is None else total + term
-        filt[pl.ds(pl.multiple_of(n * CH, 16), CH), :] = total
-
+        span = pl.ds(pl.multiple_of((tap // 9) * WIDTH, 16), 4 * WIDTH)
+        return lax.dot_general(
+            act[slot, span, :],
+            shifted[tap % 3, h],
+            (((0,), (0,)), ((), ())),
+            preferred_element_type=f32,
+        )
+
+    def inner_rows(n):
+        step_h = ((first_tap + n) // 3) % 3
+        here = pl.ds(pl.multiple_of(n * CH, 16), CH)
+        h = jnp.where(step_h == 0, 1, 0)
+        filt[here, :] = filter_term(n, h, h + step_h)
+
+        @pl.when(step_h == 1)
+        def _():
+            filt[here, :] += filter_term(n, 1, 2)
+
+    def outer_rows(n):
+        step_h = ((first_tap + n) // 3) % 3
+        here = pl.ds(pl.multiple_of(n * CH, 16), CH)
+
+        @pl.when(step_h != 1)
+        def _():
+            h = jnp.where(step_h == 0, 0, 1)
+            filt[here, :] += filter_term(n, h, h + step_h)
+
+    pl.loop(0, held // 2)(inner_rows)
+
+    @pl.when(has_before)
+    def _():
+        arrived(0, 0, tm)
+        before.start()
+        unpack(0, 0, tm)
+
+    @pl.when(has_after)
+    def _():
+        arrived(0, 3, tm)
+        after.start()
+        unpack(0, 3, tm)
+
+    pl.loop(held // 2, held)(inner_rows)
+
+    @pl.when(has_before)
+    def _():
+        arrived(0, 0, 1 - tm)
+        unpack(0, 0, 1 - tm)
+
+    @pl.when(has_after)
+    def _():
+        arrived(0, 3, 1 - tm)
+        unpack(0, 3, 1 - tm)
+
+    pl.loop(0, held)(outer_rows)
+
+    tall, cut = -(-chunk // 16) * 16, -(-chunk // 32) * 16
     for q in range(4):
 
         @pl.when(quarter == q)
         def _():
-            base = q * per_window - starts[q] * CH
             for i in range(pairs):
-                outgoing[i] = filt[base + i * chunk : base + (i + 1) * chunk, :].astype(bf16)
+                base = q * per_window - starts[q] * CH + i * chunk
+                outgoing[i, 0:chunk, :] = filt[base : base + chunk, 0:128].astype(bf16)
+                outgoing[i, tall : tall + cut, 0:64] = filt[base : base + cut, 128:CH].astype(bf16)
+                outgoing[i, tall : tall + chunk - cut, 64:128] = filt[
+                    base + cut : base + chunk, 128:CH
+                ].astype(bf16)
 
     pieces = []
     for i in range(pairs):
@@ -249,12 +303,20 @@
         def _():
             incoming[pair] = outgoing[i]
 
-    @pl.when(has_outer_cot(pair, side, pairs))
+    @pl.when(has_outer)
+    def _():
+        arrived(1, cot_slot, tm)
+        edge.start()
+        unpack(1, cot_slot, tm)
+
+    convolve(2 - 2 * side, 2 * side, False)
+
+    @pl.when(has_outer)
     def _():
         arrived(1, cot_slot, 1 - tm)
-
-    convolve(0, False)
-    convolve(2, False)
+        unpack(1, cot_slot, 1 - tm)
+
+    convolve(2 * side, 2 - 2 * side, False)
 
     for frame in range(2):
         span = pl.ds(frame * WIDTH, WIDTH)
@@ -289,7 +351,10 @@
     total = incoming[0].astype(f32)
     for source in range(1, pairs):
         total = total + incoming[source].astype(f32)
-    fg_ref[...] = (total / scale).astype(bf16)
+    total = (total / scale).astype(bf16)
+    fg_ref[:, 0:128] = total[0:chunk]
+    fg_ref[0:cut, 128:CH] = total[tall : tall + cut, 0:64]
+    fg_ref[cut:chunk, 128:CH] = total[tall : tall + chunk - cut, 64:128]
 
     for copy in straight + onward:
         copy.wait_send()
@@ -313,11 +378,6 @@
         @pl.when(owner != row)
         def _():
             piece.wait_send()
-
-
-def has_outer_cot(pair, side, pairs):
-    outer = pair + 2 * side - 1
-    return jnp.logical_and(outer >= 0, outer < pairs)
 
 
 def fused(inputs, weight, cotangent):
@@ -330,6 +390,7 @@
     held = max(
         -(-(q + 1) * quarter_rows // CH) - q * quarter_rows // CH for q in range(4)
     )
+    piece_rows = -(-chunk // 16) * 16 + -(-chunk // 32) * 16
     vmem = pl.BlockSpec(memory_space=pltpu.VMEM)
     bf16, f32 = jnp.bfloat16, jnp.float32
     out, ig, fg = pl.pallas_call(
@@ -339,18 +400,22 @@
             jax.ShapeDtypeStruct((BLOCK, CH), bf16),
             jax.ShapeDtypeStruct((chunk, CH), bf16),
         ),
-        in_specs=[vmem] * 3,
+        in_specs=[vmem, pl.BlockSpec(memory_space=pl.ANY), vmem],
         out_specs=(vmem, vmem, vmem),
         scratch_shapes=[
             pltpu.VMEM((4, 3 * BLOCK, CH), bf16),
             pltpu.VMEM((4, 3 * BLOCK, CH), bf16),
+            pltpu.VMEM((2, 4, 2, PACKED, 128), bf16),
+            pltpu.VMEM((CH, TAPS * CH), bf16),
+            pltpu.VMEM((TAPS, CH, CH), bf16),
             pltpu.VMEM((3, 2, 2 * BLOCK, CH), bf16),
             pltpu.VMEM((held * CH, CH), f32),
-            pltpu.VMEM((pairs, chunk, CH), bf16),
-            pltpu.VMEM((pairs, chunk, CH), bf16),
+            pltpu.VMEM((pairs, piece_rows, 128), bf16),
+            pltpu.VMEM((pairs, piece_rows, 128), bf16),
             pltpu.VMEM((3, BLOCK, CH), f32),
             pltpu.VMEM((3, BLOCK, CH), f32),
             pltpu.VMEM((WIDTH + 16, CH), f32),
+            pltpu.SemaphoreType.DMA,
             pltpu.SemaphoreType.DMA((12,)),
             pltpu.SemaphoreType.DMA((2, 4, 2)),
             pltpu.SemaphoreType.DMA((pairs,)),
@@ -359,7 +424,7 @@
         compiler_params=pltpu.CompilerParams(
             collective_id=0, has_side_effects=True, vmem_limit_bytes=48 * 1024 * 1024
         ),
-    )(inputs.reshape(BLOCK, CH), weight, cotangent.reshape(BLOCK, CH))
+    )(inputs.reshape(BLOCK, CH), weight.T, cotangent.reshape(BLOCK, CH))
     shape = (frames, rows, WIDTH * CH)
     return out.reshape(shape), ig.reshape(shape), fg.reshape(-1)
 
@@ -451,7 +516,7 @@
 
 def either(mesh, inputs, weight, cotangent):
     size = mesh.shape["row"]
-    quads = mesh.shape["tm"] == 2 and size % 2 == 0 and TAPS * CH % (2 * size) == 0
+    quads = mesh.shape["tm"] == 2 and size % 2 == 0 and TAPS * CH % (4 * size) == 0
     if quads and inputs.shape[:2] == (2, 1):
         return fused(inputs, weight, cotangent)
     return on_device(inputs, weight, cotangent)

time: 60.3 us -> 47.2 us (0.78)
  Pallas kernels: 48.8 us -> 39.6 us
  local copies, waits for them, and re-layouts: 10.6 us -> 6.67 us
    pallas_call x1, Pallas kernels: 48.8 us -> 39.6 us  [fused(): pl.pallas_call(functools.partial(fused_kernel, pairs, chunk, float(scale)...]
    unnamed x3 -> x2, local copies, waits for them, and re-layouts: 4.53 us -> 1.56 us
    reshape x3, local copies, waits for them, and re-layouts: 3.73 us -> 2.79 us  [fused(): return (out.reshape(shape), ig.reshape(shape), fg.reshape(-1))]
where the time goes in v2:
time: 47.2 us; the launch traced here: 47 us
  Pallas kernels  39.6 us (84%)
  local copies, waits for them, and re-layouts  6.67 us (14%)
  between operations  0.66 us (1%)
    pallas_call x1, Pallas kernels, fused(): pl.pallas_call(functools.partial(fused_kernel, pairs, chunk, float(scale)...  39.6 us
    reshape x3, local copies, waits for them, and re-layouts, fused(): return (out.reshape(shape), ig.reshape(shape), fg.reshape(-1))  2.79 us
    unnamed x2, local copies, waits for them, and re-layouts  1.56 us
    reshape x1, local copies, waits for them, and re-layouts, fused(): cotangent.reshape(BLOCK, CH)  1.17 us
    reshape x1, local copies, waits for them, and re-layouts, fused(): inputs.reshape(BLOCK, CH)  1.16 us

profile of v2, /device:TPU:31, one launch (start us, length us, event | category | flops | bytes accessed | tf_op | source)
XLA Modules:
  0.0 47.0 jit_solution(10115786381574447513)
XLA Ops:
  0.6 1.2 %reshape.21.x_ref = bf16[448,192]{1,0:T(8,128)(2,1)S(1)} reshape(bf16[2,1,43008]{2,0,1:T(2,128)(2,1)} %param.3) | data formatting | bytes 344064 | tf_op jit(solution)/shard_map/reshape | solution.py:427
  1.8 1.2 %reshape.22.c_ref = bf16[448,192]{1,0:T(8,128)(2,1)S(1)} reshape(bf16[2,1,43008]{2,0,1:T(2,128)(2,1)} %param.5) | data formatting | bytes 344064 | tf_op jit(solution)/shard_map/reshape | solution.py:427
  3.0 0.0 copy-start
  3.0 1.6 %copy-done = bf16[5184,192]{0,1:T(8,128)(2,1)S(1)} copy-done((bf16[5184,192]{0,1:T(8,128)(2,1)S(1)}, bf16[5184,192]{0,1:T(8,128)(2,1)}, u32[]{:S(2)}) %copy-start) | copy-done | bytes 1990680
  4.5 39.6 %shard_map.58 = (bf16[448,192]{1,0:T(8,128)(2,1)S(1)}, bf16[448,192]{1,0:T(8,128)(2,1)S(1)}, bf16[324,192]{1,0:T(8,128)(2,1)S(1)}) custom-call(bf16[448,192]{1,0:T(8,128)(2,1)S(1)} %reshape.21.x_ref, bf16[192,5184]{1,0:T(8,128)(2,1)S(1)} %bitcast.5, bf16[448,192]{1,0:T(8,128)(2,1)S(1)} %reshape.22.c_ref), custom_call_target="tpu_custom_call" | custom-call | tf_op jit(solution)/shard_map/pallas_call | solution.py:396
  44.2 1.0 %reshape.23 = bf16[2,1,43008]{2,0,1:T(2,128)(2,1)} reshape(bf16[448,192]{1,0:T(8,128)(2,1)S(1)} %get-tuple-element.6) | data formatting | bytes 344064 | tf_op jit(solution)/shard_map/reshape | solution.py:429
  45.1 0.9 %reshape.25 = bf16[62208]{0:T(1024)(128)(2,1)} reshape(bf16[324,192]{1,0:T(8,128)(2,1)S(1)} %get-tuple-element.8) | data formatting | bytes 248832 | tf_op jit(solution)/shard_map/reshape | solution.py:429
  46.0 1.0 %reshape.24 = bf16[2,1,43008]{2,0,1:T(2,128)(2,1)} reshape(bf16[448,192]{1,0:T(8,128)(2,1)S(1)} %get-tuple-element.7) | data formatting | bytes 344064 | tf_op jit(solution)/shard_map/reshape | solution.py:429
Async XLA Ops:
  3.0 1.6 %copy-start = (bf16[5184,192]{0,1:T(8,128)(2,1)S(1)}, bf16[5184,192]{0,1:T(8,128)(2,1)}, u32[]{:S(2)}) copy-start(bf16[5184,192]{0,1:T(8,128)(2,1)} %param.4) | copy-start | bytes 5971972

commit v3 on v2

--- a/solution.py
+++ b/solution.py
@@ -84,10 +84,10 @@
     cot_slot = 3 * side
     has_before, has_after = pair > 0, pair < pairs - 1
 
-    x = x_ref[...].astype(f32)
-    value = (x * (1.0 / (1.0 + jnp.exp(-x)))).astype(bf16)
-    act[own, pl.ds(pl.multiple_of((tm + 1) * BLOCK, 16), BLOCK), :] = value
-    pack(0, own, tm, value)
+    inner_pair = pair + 1 - 2 * side
+    has_same = jnp.logical_and(inner_pair >= 0, inner_pair < pairs)
+    cross_slot, same_slot = cot_slot, outer_slot
+
     value = c_ref[...]
     cot[own, pl.ds(pl.multiple_of(tm * BLOCK, 16), BLOCK), :] = value
     pack(1, own, tm, value)
@@ -104,16 +104,18 @@
         move(0, own, outer_slot, tm, 6, outer_same),
         move(1, own, outer_slot, tm, 5, outer_cross),
     ]
-    for copy in straight[:2]:
-        copy.start()
+    straight[1].start()
+    straight[3].start()
+    x = x_ref[...].astype(f32)
+    value = (x * (1.0 / (1.0 + jnp.exp(-x)))).astype(bf16)
+    act[own, pl.ds(pl.multiple_of((tm + 1) * BLOCK, 16), BLOCK), :] = value
+    pack(0, own, tm, value)
+    straight[0].start()
+    straight[2].start()
 
     @pl.when(has_outer)
     def _():
-        for copy in outward[:2]:
-            copy.start()
-
-    for copy in straight[2:]:
-        copy.start()
+        outward[1].start()
 
     for slot in range(4):
         act[slot, 0:BLOCK, :] = jnp.zeros((BLOCK, CH), bf16)
@@ -186,16 +188,23 @@
     shift(side)
 
     onward = [move(0, other_slot, other_slot, tm, 7, sibling), move(1, other_slot, other_slot, tm, 8, sibling)]
-    before = move(0, 0, 0, tm, 9, sibling)
-    after = move(0, 3, 3, tm, 10, sibling)
+    same = move(0, same_slot, same_slot, tm, 9, sibling)
+    cross = move(0, cross_slot, cross_slot, tm, 10, sibling)
     edge = move(1, cot_slot, cot_slot, tm, 11, sibling)
-    for array in range(2):
+    for array in (1, 0):
         arrived(array, other_slot, tm)
         onward[array].start()
 
     @pl.when(has_outer)
     def _():
+        outward[0].start()
         outward[2].start()
+
+    @pl.when(has_same)
+    def _():
+        arrived(0, same_slot, tm)
+        same.start()
+        unpack(0, same_slot, tm)
 
     for array in range(2):
         unpack(array, other_slot, tm)
@@ -232,42 +241,32 @@
         def _():
             filt[here, :] += filter_term(n, 1, 2)
 
-    def outer_rows(n):
+    def outer_rows(slot, n):
         step_h = ((first_tap + n) // 3) % 3
         here = pl.ds(pl.multiple_of(n * CH, 16), CH)
 
-        @pl.when(step_h != 1)
-        def _():
-            h = jnp.where(step_h == 0, 0, 1)
-            filt[here, :] += filter_term(n, h, h + step_h)
-
-    pl.loop(0, held // 2)(inner_rows)
-
-    @pl.when(has_before)
-    def _():
-        arrived(0, 0, tm)
-        before.start()
-        unpack(0, 0, tm)
-
-    @pl.when(has_after)
-    def _():
-        arrived(0, 3, tm)
-        after.start()
-        unpack(0, 3, tm)
-
-    pl.loop(held // 2, held)(inner_rows)
-
-    @pl.when(has_before)
-    def _():
-        arrived(0, 0, 1 - tm)
-        unpack(0, 0, 1 - tm)
-
-    @pl.when(has_after)
-    def _():
-        arrived(0, 3, 1 - tm)
-        unpack(0, 3, 1 - tm)
-
-    pl.loop(0, held)(outer_rows)
+        @pl.when(step_h == jnp.where(slot == 0, 0, 2))
+        def _():
+            filt[here, :] += filter_term(n, slot // 3, slot)
+
+    pl.loop(0, held)(inner_rows)
+
+    @pl.when(has_same)
+    def _():
+        arrived(0, same_slot, 1 - tm)
+        unpack(0, same_slot, 1 - tm)
+
+    pl.loop(0, held)(functools.partial(outer_rows, same_slot))
+
+    @pl.when(has_outer)
+    def _():
+        arrived(0, cross_slot, tm)
+        cross.start()
+        unpack(0, cross_slot, tm)
+        arrived(0, cross_slot, 1 - tm)
+        unpack(0, cross_slot, 1 - tm)
+
+    pl.loop(0, held)(functools.partial(outer_rows, cross_slot))
 
     tall, cut = -(-chunk // 16) * 16, -(-chunk // 32) * 16
     for q in range(4):
@@ -364,14 +363,11 @@
         for copy in outward:
             copy.wait_send()
         edge.wait_send()
-
-    @pl.when(has_before)
-    def _():
-        before.wait_send()
-
-    @pl.when(has_after)
-    def _():
-        after.wait_send()
+        cross.wait_send()
+
+    @pl.when(has_same)
+    def _():
+        same.wait_send()
 
     for owner, piece in pieces:
 
@@ -400,7 +396,7 @@
             jax.ShapeDtypeStruct((BLOCK, CH), bf16),
             jax.ShapeDtypeStruct((chunk, CH), bf16),
         ),
-        in_specs=[vmem, pl.BlockSpec(memory_space=pl.ANY), vmem],
+        in_specs=[vmem, pl.BlockSpec(memory_space=pltpu.HBM), vmem],
         out_specs=(vmem, vmem, vmem),
         scratch_shapes=[
             pltpu.VMEM((4, 3 * BLOCK, CH), bf16),

time: 47.2 us -> 45.3 us (0.960)
  Pallas kernels: 39.6 us -> 37.7 us
    pallas_call x1, Pallas kernels: 39.6 us -> 37.7 us  [fused(): pl.pallas_call(functools.partial(fused_kernel, pairs, chunk, float(scale)...]
where the time goes in v3:
time: 45.3 us; the launch traced here: 45.1 us
  Pallas kernels  37.7 us (83%)
  local copies, waits for them, and re-layouts  6.67 us (15%)
  between operations  0.66 us (1%)
    pallas_call x1, Pallas kernels, fused(): pl.pallas_call(functools.partial(fused_kernel, pairs, chunk, float(scale)...  37.7 us
    reshape x3, local copies, waits for them, and re-layouts, fused(): return (out.reshape(shape), ig.reshape(shape), fg.reshape(-1))  2.79 us
    unnamed x2, local copies, waits for them, and re-layouts  1.56 us
    reshape x1, local copies, waits for them, and re-layouts, fused(): cotangent.reshape(BLOCK, CH)  1.17 us
    reshape x1, local copies, waits for them, and re-layouts, fused(): inputs.reshape(BLOCK, CH)  1.16 us

profile of v3, /device:TPU:31, one launch (start us, length us, event | category | flops | bytes accessed | tf_op | source)
XLA Modules:
  0.0 45.1 jit_solution(14584561520293033960)
XLA Ops:
  0.6 1.2 %reshape.21.x_ref = bf16[448,192]{1,0:T(8,128)(2,1)S(1)} reshape(bf16[2,1,43008]{2,0,1:T(2,128)(2,1)} %param.3) | data formatting | bytes 344064 | tf_op jit(solution)/shard_map/reshape | solution.py:423
  1.8 1.2 %reshape.22.c_ref = bf16[448,192]{1,0:T(8,128)(2,1)S(1)} reshape(bf16[2,1,43008]{2,0,1:T(2,128)(2,1)} %param.5) | data formatting | bytes 344064 | tf_op jit(solution)/shard_map/reshape | solution.py:423
  3.0 0.0 copy-start
  3.0 1.6 %copy-done = bf16[5184,192]{0,1:T(8,128)(2,1)S(1)} copy-done((bf16[5184,192]{0,1:T(8,128)(2,1)S(1)}, bf16[5184,192]{0,1:T(8,128)(2,1)}, u32[]{:S(2)}) %copy-start) | copy-done | bytes 1990680
  4.5 37.7 %shard_map.58 = (bf16[448,192]{1,0:T(8,128)(2,1)S(1)}, bf16[448,192]{1,0:T(8,128)(2,1)S(1)}, bf16[324,192]{1,0:T(8,128)(2,1)S(1)}) custom-call(bf16[448,192]{1,0:T(8,128)(2,1)S(1)} %reshape.21.x_ref, bf16[192,5184]{1,0:T(8,128)(2,1)S(1)} %bitcast.5, bf16[448,192]{1,0:T(8,128)(2,1)S(1)} %reshape.22.c_ref), custom_call_target="tpu_custom_call" | custom-call | tf_op jit(solution)/shard_map/pallas_call | solution.py:392
  42.3 1.0 %reshape.23 = bf16[2,1,43008]{2,0,1:T(2,128)(2,1)} reshape(bf16[448,192]{1,0:T(8,128)(2,1)S(1)} %get-tuple-element.6) | data formatting | bytes 344064 | tf_op jit(solution)/shard_map/reshape | solution.py:425
  43.3 0.9 %reshape.25 = bf16[62208]{0:T(1024)(128)(2,1)} reshape(bf16[324,192]{1,0:T(8,128)(2,1)S(1)} %get-tuple-element.8) | data formatting | bytes 248832 | tf_op jit(solution)/shard_map/reshape | solution.py:425
  44.1 1.0 %reshape.24 = bf16[2,1,43008]{2,0,1:T(2,128)(2,1)} reshape(bf16[448,192]{1,0:T(8,128)(2,1)S(1)} %get-tuple-element.7) | data formatting | bytes 344064 | tf_op jit(solution)/shard_map/reshape | solution.py:425
Async XLA Ops:
  3.0 1.6 %copy-start = (bf16[5184,192]{0,1:T(8,128)(2,1)S(1)}, bf16[5184,192]{0,1:T(8,128)(2,1)}, u32[]{:S(2)}) copy-start(bf16[5184,192]{0,1:T(8,128)(2,1)} %param.4) | copy-start | bytes 5971972

commit v4 on v3

--- a/solution.py
+++ b/solution.py
@@ -268,19 +268,6 @@
 
     pl.loop(0, held)(functools.partial(outer_rows, cross_slot))
 
-    tall, cut = -(-chunk // 16) * 16, -(-chunk // 32) * 16
-    for q in range(4):
-
-        @pl.when(quarter == q)
-        def _():
-            for i in range(pairs):
-                base = q * per_window - starts[q] * CH + i * chunk
-                outgoing[i, 0:chunk, :] = filt[base : base + chunk, 0:128].astype(bf16)
-                outgoing[i, tall : tall + cut, 0:64] = filt[base : base + cut, 128:CH].astype(bf16)
-                outgoing[i, tall : tall + chunk - cut, 64:128] = filt[
-                    base + cut : base + chunk, 128:CH
-                ].astype(bf16)
-
     pieces = []
     for i in range(pairs):
         owner = window * pairs + i
@@ -294,13 +281,27 @@
         )
         pieces.append((owner, piece))
 
-        @pl.when(owner != row)
+    tall, cut = -(-chunk // 16) * 16, -(-chunk // 32) * 16
+    for q in range(4):
+
+        @pl.when(quarter == q)
         def _():
-            piece.start()
-
-        @pl.when(owner == row)
-        def _():
-            incoming[pair] = outgoing[i]
+            for i in range(pairs):
+                base = q * per_window - starts[q] * CH + i * chunk
+                outgoing[i, 0:chunk, :] = filt[base : base + chunk, 0:128].astype(bf16)
+                outgoing[i, tall : tall + cut, 0:64] = filt[base : base + cut, 128:CH].astype(bf16)
+                outgoing[i, tall : tall + chunk - cut, 64:128] = filt[
+                    base + cut : base + chunk, 128:CH
+                ].astype(bf16)
+                owner, piece = pieces[i]
+
+                @pl.when(owner != row)
+                def _():
+                    piece.start()
+
+                @pl.when(owner == row)
+                def _():
+                    incoming[pair] = outgoing[i]
 
     @pl.when(has_outer)
     def _():

time: 45.3 us -> 45.2 us (level)
  no operation moved by 1% of the time
where the time goes in v4:
time: 45.2 us; the launch traced here: 45 us
  Pallas kernels  37.7 us (83%)
  local copies, waits for them, and re-layouts  6.67 us (15%)
  between operations  0.66 us (1%)
    pallas_call x1, Pallas kernels, fused(): pl.pallas_call(functools.partial(fused_kernel, pairs, chunk, float(scale)...  37.7 us
    reshape x3, local copies, waits for them, and re-layouts, fused(): return (out.reshape(shape), ig.reshape(shape), fg.reshape(-1))  2.79 us
    unnamed x2, local copies, waits for them, and re-layouts  1.56 us
    reshape x1, local copies, waits for them, and re-layouts, fused(): cotangent.reshape(BLOCK, CH)  1.17 us
    reshape x1, local copies, waits for them, and re-layouts, fused(): inputs.reshape(BLOCK, CH)  1.16 us

profile of v4, /device:TPU:31, one launch (start us, length us, event | category | flops | bytes accessed | tf_op | source)
XLA Modules:
  0.0 45.0 jit_solution(15959380535317369702)
XLA Ops:
  0.6 1.2 %reshape.21.x_ref = bf16[448,192]{1,0:T(8,128)(2,1)S(1)} reshape(bf16[2,1,43008]{2,0,1:T(2,128)(2,1)} %param.3) | data formatting | bytes 344064 | tf_op jit(solution)/shard_map/reshape | solution.py:424
  1.8 1.2 %reshape.22.c_ref = bf16[448,192]{1,0:T(8,128)(2,1)S(1)} reshape(bf16[2,1,43008]{2,0,1:T(2,128)(2,1)} %param.5) | data formatting | bytes 344064 | tf_op jit(solution)/shard_map/reshape | solution.py:424
  3.0 0.0 copy-start
  3.0 1.6 %copy-done = bf16[5184,192]{0,1:T(8,128)(2,1)S(1)} copy-done((bf16[5184,192]{0,1:T(8,128)(2,1)S(1)}, bf16[5184,192]{0,1:T(8,128)(2,1)}, u32[]{:S(2)}) %copy-start) | copy-done | bytes 1990680
  4.5 37.7 %shard_map.58 = (bf16[448,192]{1,0:T(8,128)(2,1)S(1)}, bf16[448,192]{1,0:T(8,128)(2,1)S(1)}, bf16[324,192]{1,0:T(8,128)(2,1)S(1)}) custom-call(bf16[448,192]{1,0:T(8,128)(2,1)S(1)} %reshape.21.x_ref, bf16[192,5184]{1,0:T(8,128)(2,1)S(1)} %bitcast.5, bf16[448,192]{1,0:T(8,128)(2,1)S(1)} %reshape.22.c_ref), custom_call_target="tpu_custom_call" | custom-call | tf_op jit(solution)/shard_map/pallas_call | solution.py:393
  42.2 1.0 %reshape.23 = bf16[2,1,43008]{2,0,1:T(2,128)(2,1)} reshape(bf16[448,192]{1,0:T(8,128)(2,1)S(1)} %get-tuple-element.6) | data formatting | bytes 344064 | tf_op jit(solution)/shard_map/reshape | solution.py:426
  43.2 0.9 %reshape.25 = bf16[62208]{0:T(1024)(128)(2,1)} reshape(bf16[324,192]{1,0:T(8,128)(2,1)S(1)} %get-tuple-element.8) | data formatting | bytes 248832 | tf_op jit(solution)/shard_map/reshape | solution.py:426
  44.1 1.0 %reshape.24 = bf16[2,1,43008]{2,0,1:T(2,128)(2,1)} reshape(bf16[448,192]{1,0:T(8,128)(2,1)S(1)} %get-tuple-element.7) | data formatting | bytes 344064 | tf_op jit(solution)/shard_map/reshape | solution.py:426
Async XLA Ops:
  3.0 1.6 %copy-start = (bf16[5184,192]{0,1:T(8,128)(2,1)S(1)}, bf16[5184,192]{0,1:T(8,128)(2,1)}, u32[]{:S(2)}) copy-start(bf16[5184,192]{0,1:T(8,128)(2,1)} %param.4) | copy-start | bytes 5971972

commit v5 on v4

--- a/solution.py
+++ b/solution.py
@@ -263,6 +263,11 @@
         arrived(0, cross_slot, tm)
         cross.start()
         unpack(0, cross_slot, tm)
+
+    convolve(2 - 2 * side, 2 * side, False)
+
+    @pl.when(has_outer)
+    def _():
         arrived(0, cross_slot, 1 - tm)
         unpack(0, cross_slot, 1 - tm)
 
@@ -308,8 +313,6 @@
         arrived(1, cot_slot, tm)
         edge.start()
         unpack(1, cot_slot, tm)
-
-    convolve(2 - 2 * side, 2 * side, False)
 
     @pl.when(has_outer)
     def _():

time: 45.2 us -> 44.1 us (0.976)
  Pallas kernels: 37.7 us -> 36.5 us
    pallas_call x1, Pallas kernels: 37.7 us -> 36.5 us  [fused(): pl.pallas_call(functools.partial(fused_kernel, pairs, chunk, float(scale)...]
where the time goes in v5:
time: 44.1 us; the launch traced here: 43.8 us
  Pallas kernels  36.5 us (83%)
  local copies, waits for them, and re-layouts  6.67 us (15%)
  between operations  0.66 us (1%)
    pallas_call x1, Pallas kernels, fused(): pl.pallas_call(functools.partial(fused_kernel, pairs, chunk, float(scale)...  36.5 us
    reshape x3, local copies, waits for them, and re-layouts, fused(): return (out.reshape(shape), ig.reshape(shape), fg.reshape(-1))  2.79 us
    unnamed x2, local copies, waits for them, and re-layouts  1.56 us
    reshape x1, local copies, waits for them, and re-layouts, fused(): cotangent.reshape(BLOCK, CH)  1.17 us
    reshape x1, local copies, waits for them, and re-layouts, fused(): inputs.reshape(BLOCK, CH)  1.16 us

profile of v5, /device:TPU:31, one launch (start us, length us, event | category | flops | bytes accessed | tf_op | source)
XLA Modules:
  0.0 43.8 jit_solution(7075936401978418121)
XLA Ops:
  0.6 1.2 %reshape.21.x_ref = bf16[448,192]{1,0:T(8,128)(2,1)S(1)} reshape(bf16[2,1,43008]{2,0,1:T(2,128)(2,1)} %param.3) | data formatting | bytes 344064 | tf_op jit(solution)/shard_map/reshape | solution.py:427
  1.8 1.2 %reshape.22.c_ref = bf16[448,192]{1,0:T(8,128)(2,1)S(1)} reshape(bf16[2,1,43008]{2,0,1:T(2,128)(2,1)} %param.5) | data formatting | bytes 344064 | tf_op jit(solution)/shard_map/reshape | solution.py:427
  3.0 0.0 copy-start
  3.0 1.6 %copy-done = bf16[5184,192]{0,1:T(8,128)(2,1)S(1)} copy-done((bf16[5184,192]{0,1:T(8,128)(2,1)S(1)}, bf16[5184,192]{0,1:T(8,128)(2,1)}, u32[]{:S(2)}) %copy-start) | copy-done | bytes 1990680
  4.5 36.5 %shard_map.58 = (bf16[448,192]{1,0:T(8,128)(2,1)S(1)}, bf16[448,192]{1,0:T(8,128)(2,1)S(1)}, bf16[324,192]{1,0:T(8,128)(2,1)S(1)}) custom-call(bf16[448,192]{1,0:T(8,128)(2,1)S(1)} %reshape.21.x_ref, bf16[192,5184]{1,0:T(8,128)(2,1)S(1)} %bitcast.5, bf16[448,192]{1,0:T(8,128)(2,1)S(1)} %reshape.22.c_ref), custom_call_target="tpu_custom_call" | custom-call | tf_op jit(solution)/shard_map/pallas_call | solution.py:396
  41.0 1.0 %reshape.23 = bf16[2,1,43008]{2,0,1:T(2,128)(2,1)} reshape(bf16[448,192]{1,0:T(8,128)(2,1)S(1)} %get-tuple-element.6) | data formatting | bytes 344064 | tf_op jit(solution)/shard_map/reshape | solution.py:429
  42.0 0.9 %reshape.25 = bf16[62208]{0:T(1024)(128)(2,1)} reshape(bf16[324,192]{1,0:T(8,128)(2,1)S(1)} %get-tuple-element.8) | data formatting | bytes 248832 | tf_op jit(solution)/shard_map/reshape | solution.py:429
  42.9 1.0 %reshape.24 = bf16[2,1,43008]{2,0,1:T(2,128)(2,1)} reshape(bf16[448,192]{1,0:T(8,128)(2,1)S(1)} %get-tuple-element.7) | data formatting | bytes 344064 | tf_op jit(solution)/shard_map/reshape | solution.py:429
Async XLA Ops:
  3.0 1.6 %copy-start = (bf16[5184,192]{0,1:T(8,128)(2,1)S(1)}, bf16[5184,192]{0,1:T(8,128)(2,1)}, u32[]{:S(2)}) copy-start(bf16[5184,192]{0,1:T(8,128)(2,1)} %param.4) | copy-start | bytes 5971972
